TPU v7x, 512 devices: a whole 4x8x8 slice. The times are simulated.
512 devices in a mesh: seq: 64 (over y, x, core), head: 8 (over z).
Axes of the slice: x: 4, y: 8, z: 8, core: 2. Of those that a mesh axis runs over, the one named last changes fastest.
Arguments:
- queries: bfloat16 [8192, 4096], P('seq', 'head'), may hold values from -0.71875 to 0.71875
- key_rows: bfloat16 [8192, 4096], P('seq', 'head'), may hold values from -0.71875 to 0.71875
- value_rows: bfloat16 [8192, 4096], P('seq', 'head'), may hold values from -0.71875 to 0.71875
- segment_ids: int32 [8192], P('seq'), may hold values from 0 to 7, never falling along the last dimension, each value on 1 to 2048 neighbouring positions
- decay_span: float32 [32], P('head'), may hold values from 30 to 81920, as said below
- norm_gain: float32 [4096], P('head'), may hold values from 0.5 to 1.5
- out_grad: bfloat16 [8192, 4096], P('seq', 'head'), may hold values from -0.71875 to 0.71875
Outputs:
- query_grad: bfloat16 [8192, 4096], P('seq', 'head')
- key_grad: bfloat16 [8192, 4096], P('seq', 'head')
- value_grad: bfloat16 [8192, 4096], P('seq', 'head')
- gain_grad: float32 [4096], P('head')
Inputs may be any that keep to these rules, and one draw needn't show every extreme that they name: segment_ids never falls along the segment; every document of the 8 has a token and the longest has 2048. The decay per token of head h is exp(-1 / decay_span[h]).
All inputs are finite; a program needn't handle non-finite values.
Results may differ from a plain program's by a relative error of at most 0.0012.
Values sent between devices are 32-bit elements; how exact they have to be, the bound alone decides.
A program may use at most 64 MiB of HBM per device.

v0:
```python
import jax
import jax.numpy as jnp
from jax import lax
from jax.sharding import PartitionSpec as P

HEADS = 32
HEAD_DIM = 128
exact = lax.Precision.HIGHEST


def prefix_2(part, axis, combine, identity, reverse):
    count = lax.axis_size(axis)
    place = lax.axis_index(axis)
    ahead = count - 1 - place if reverse else place
    gathered = jax.tree.map(lambda a: lax.all_gather(a, axis), part)
    state = jax.tree.map(lambda a, e: jnp.zeros_like(a) + jnp.asarray(e, a.dtype), part, identity)

    def one(step, state):
        source = count - 1 - step if reverse else step
        return combine(
            state, jax.tree.map(lambda a: lax.dynamic_index_in_dim(a, source, 0, False), gathered)
        )

    return lax.fori_loop(0, ahead, one, state)


def combine_forward(earlier, later):
    state_early, decay_early, first_early, last_early = earlier
    state_late, decay_late, first_late, last_late = later
    passes = jnp.logical_or(
        jnp.logical_and(first_late == last_late, first_late == last_early), first_late < 0
    )
    factor = jnp.where(passes, decay_late, 0.0)
    return (
        state_late + factor[:, None, None] * state_early,
        decay_early * decay_late,
        jnp.where(first_early < 0, first_late, first_early),
        jnp.where(last_late < 0, last_early, last_late),
    )


def combine_backward(earlier, later):
    state_high, decay_high, first_high, last_high = earlier
    state_low, decay_low, first_low, last_low = later
    passes = jnp.logical_or(
        jnp.logical_and(first_low == last_low, last_low == first_high), first_low < 0
    )
    factor = jnp.where(passes, decay_low, 0.0)
    return (
        state_low + factor[:, None, None] * state_high,
        decay_high * decay_low,
        jnp.where(first_low < 0, first_high, first_low),
        jnp.where(last_high < 0, last_low, last_high),
    )


def local(queries, key_rows, value_rows, segment_ids, decay_span, norm_gain, out_grad):
    tok_rows = queries.shape[0]
    heads_here = decay_span.shape[0]
    all_features = HEADS * HEAD_DIM
    block_rows = min(tok_rows, 512)
    block_count = tok_rows // block_rows
    seg_float = segment_ids.astype(jnp.float32)
    positions = jnp.arange(tok_rows, dtype=jnp.float32)
    first_seg = seg_float[0]
    last_seg = seg_float[-1]
    query_full = queries.reshape(tok_rows, heads_here, HEAD_DIM).astype(jnp.float32)
    key_full = key_rows.reshape(tok_rows, heads_here, HEAD_DIM).astype(jnp.float32)
    value_full = value_rows.reshape(tok_rows, heads_here, HEAD_DIM).astype(jnp.float32)
    shard_decay = jnp.exp(-tok_rows / decay_span)
    tail_on = jnp.where(
        (seg_float == last_seg)[:, None],
        jnp.exp(-(tok_rows - 1.0 - positions)[:, None] / decay_span[None, :]),
        0.0,
    )
    local_state = jnp.einsum(
        "thi,thj->hij", key_full * tail_on[:, :, None], value_full, precision=exact
    )
    summary = (local_state, shard_decay, first_seg, last_seg)
    identity = (
        jnp.zeros_like(local_state),
        jnp.ones_like(decay_span),
        jnp.float32(-1.0),
        jnp.float32(-1.0),
    )
    prefix = prefix_2(summary, "seq", combine_forward, identity, False)
    state_in = prefix[0]
    prev_seg = prefix[3]
    offsets = jnp.arange(block_rows, dtype=jnp.float32)
    offset_gap = offsets[:, None] - offsets[None, :]
    causal = offset_gap >= 0
    decay_tile = jnp.where(
        causal[None], jnp.exp(-jnp.maximum(offset_gap, 0.0)[None] / decay_span[:, None, None]), 0.0
    )
    into_weight = jnp.exp(-(offsets + 1.0)[:, None] / decay_span[None, :])
    tail_weight = jnp.exp(-(block_rows - 1.0 - offsets)[:, None] / decay_span[None, :])
    start_weight = jnp.exp(-offsets[:, None] / decay_span[None, :])
    next_weight = jnp.exp(-(block_rows - offsets)[:, None] / decay_span[None, :])
    whole_weight = jnp.exp(-block_rows / decay_span)
    query_blocks = query_full.reshape(block_count, block_rows, heads_here, HEAD_DIM)
    key_blocks = key_full.reshape(block_count, block_rows, heads_here, HEAD_DIM)
    value_blocks = value_full.reshape(block_count, block_rows, heads_here, HEAD_DIM)
    grad_blocks = out_grad.reshape(block_count, block_rows, heads_here * HEAD_DIM)
    seg_blocks = seg_float.reshape(block_count, block_rows)

    def forward_step(carry, inputs):
        state_now, carry_seg, gain_acc = carry
        query_blk, key_blk, value_blk, dy_blk, seg_blk = inputs
        dy_full = dy_blk.astype(jnp.float32)
        same_doc = (seg_blk[:, None] == seg_blk[None, :]).astype(jnp.float32)
        weights = decay_tile * same_doc[None]
        scores = jnp.einsum("thd,shd->hts", query_blk, key_blk, precision=exact) * weights
        inter_on = jnp.where((seg_blk == carry_seg)[:, None], into_weight, 0.0)
        attended = jnp.einsum("hts,shd->thd", scores, value_blk, precision=exact)
        attended = attended + inter_on[:, :, None] * jnp.einsum(
            "thi,hij->thj", query_blk, state_now, precision=exact
        )
        flat_out = attended.reshape(block_rows, heads_here * HEAD_DIM)
        square_part = jnp.sum(flat_out * flat_out, axis=1)
        cross_part = jnp.sum(dy_full * norm_gain[None, :] * flat_out, axis=1)
        square_total, cross_total = lax.psum((square_part, cross_part), "head")
        inv_scale = lax.rsqrt(square_total / all_features + 1e-06)
        out_back = (
            norm_gain[None, :] * dy_full * inv_scale[:, None]
            - flat_out * (inv_scale * inv_scale * inv_scale * cross_total / all_features)[:, None]
        )
        gain_acc = gain_acc + jnp.sum(dy_full * flat_out * inv_scale[:, None], axis=0)
        back_heads = out_back.reshape(block_rows, heads_here, HEAD_DIM)
        grad_scores = jnp.einsum("thd,shd->hts", back_heads, value_blk, precision=exact) * weights
        query_part = jnp.einsum("hts,shd->thd", grad_scores, key_blk, precision=exact)
        query_part = query_part + inter_on[:, :, None] * jnp.einsum(
            "thj,hij->thi", back_heads, state_now, precision=exact
        )
        tail_blk = jnp.where((seg_blk == seg_blk[-1])[:, None], tail_weight, 0.0)
        passes = jnp.logical_and(seg_blk[0] == seg_blk[-1], seg_blk[0] == carry_seg)
        factor = jnp.where(passes, whole_weight, 0.0)
        new_state = (
            jnp.einsum("thi,thj->hij", key_blk * tail_blk[:, :, None], value_blk, precision=exact)
            + factor[:, None, None] * state_now
        )
        outputs = (
            back_heads,
            query_part.reshape(block_rows, heads_here * HEAD_DIM).astype(jnp.bfloat16),
        )
        return ((new_state, seg_blk[-1], gain_acc), outputs)

    start_carry = (state_in, prev_seg, jnp.zeros((heads_here * HEAD_DIM,), jnp.float32))
    forward_carry, forward_out = lax.scan(
        forward_step, start_carry, (query_blocks, key_blocks, value_blocks, grad_blocks, seg_blocks)
    )
    back_blocks = forward_out[0]
    query_grad = forward_out[1].reshape(tok_rows, heads_here * HEAD_DIM)
    gain_local = forward_carry[2]
    back_all = back_blocks.reshape(tok_rows, heads_here, HEAD_DIM)
    start_on = jnp.where(
        (seg_float == first_seg)[:, None], jnp.exp(-positions[:, None] / decay_span[None, :]), 0.0
    )
    local_grad = jnp.einsum(
        "thi,thj->hij", query_full * start_on[:, :, None], back_all, precision=exact
    )
    back_summary = (local_grad, shard_decay, first_seg, last_seg)
    suffix = prefix_2(back_summary, "seq", combine_backward, identity, True)
    grad_in = suffix[0]
    next_seg = suffix[2]

    def backward_step(carry, inputs):
        grad_state, carry_seg = carry
        query_blk, key_blk, value_blk, back_heads, seg_blk = inputs[:5]
        same_doc = (seg_blk[:, None] == seg_blk[None, :]).astype(jnp.float32)
        weights = decay_tile * same_doc[None]
        scores = jnp.einsum("thd,shd->hts", query_blk, key_blk, precision=exact) * weights
        grad_scores = jnp.einsum("thd,shd->hts", back_heads, value_blk, precision=exact) * weights
        key_part = jnp.einsum("hts,thd->shd", grad_scores, query_blk, precision=exact)
        value_part = jnp.einsum("hts,thd->shd", scores, back_heads, precision=exact)
        back_on = jnp.where((seg_blk == carry_seg)[:, None], next_weight, 0.0)
        key_part = key_part + back_on[:, :, None] * jnp.einsum(
            "hij,shj->shi", grad_state, value_blk, precision=exact
        )
        value_part = value_part + back_on[:, :, None] * jnp.einsum(
            "hij,shi->shj", grad_state, key_blk, precision=exact
        )
        start_blk = jnp.where((seg_blk == seg_blk[0])[:, None], start_weight, 0.0)
        passes = jnp.logical_and(seg_blk[0] == seg_blk[-1], seg_blk[-1] == carry_seg)
        factor = jnp.where(passes, whole_weight, 0.0)
        new_state = (
            jnp.einsum(
                "thi,thj->hij", query_blk * start_blk[:, :, None], back_heads, precision=exact
            )
            + factor[:, None, None] * grad_state
        )
        return (
            (new_state, seg_blk[0]),
            (
                key_part.reshape(block_rows, heads_here * HEAD_DIM).astype(jnp.bfloat16),
                value_part.reshape(block_rows, heads_here * HEAD_DIM).astype(jnp.bfloat16),
            ),
        )

    backward_inputs = (query_blocks, key_blocks, value_blocks, back_blocks, seg_blocks)
    _, (key_grad, value_grad) = lax.scan(
        backward_step, (grad_in, next_seg), backward_inputs, reverse=True
    )
    gain_grad = lax.psum(gain_local, "seq")
    return (
        query_grad,
        key_grad.reshape(tok_rows, heads_here * HEAD_DIM),
        value_grad.reshape(tok_rows, heads_here * HEAD_DIM),
        gain_grad,
    )


def solution(mesh):
    in_specs = (
        P("seq", "head"),
        P("seq", "head"),
        P("seq", "head"),
        P("seq"),
        P("head"),
        P("head"),
        P("seq", "head"),
    )
    out_specs = (P("seq", "head"), P("seq", "head"), P("seq", "head"), P("head"))
    return jax.shard_map(local, mesh=mesh, in_specs=in_specs, out_specs=out_specs, check_vma=False)
```

profile of v0, /device:TPU:64, one launch (start us, length us, event | category | flops | bytes accessed | tf_op | source)
XLA Modules:
  0.0 1051.4 jit_solution(12014305828025439504)
XLA Ops:
  9.0 1.3 dynamic-slice.3
  10.3 1.2 fusion.42
  11.5 2.0 broadcast_compare_fusion.1
  18.4 131.0 %all-reduce.3 = (f32[64]{0:T(128)S(1)}, f32[64]{0:T(128)S(1)}, f32[256]{0:T(256)S(1)}) all-reduce(f32[64]{0:T(128)S(1)} %slice_dynamic-update-slice_fusion, f32[64]{0:T(128)S(1)} %get-tuple-element.353, f32[256]{0:T(256)S(1)} %exponential_dynamic-update-slice_fusion), channel_id=1, replica_groups=mesh['seq'=64,'head'=8] {'seq'}, use_global_device_ids=true, to_apply=%add | all-reduce | flops 384 | bytes 3072
  150.7 1.1 convolution_multiply_fusion.1
  154.1 20.0 %psum.23 = f32[128]{0:T(128)S(1)} all-reduce(f32[128]{0:T(128)S(1)} %get-tuple-element.355), channel_id=1, replica_groups=mesh['seq'=64,'head'=8] {'head'}, use_global_device_ids=true, to_apply=%region_3.4 | all-reduce | flops 128 | bytes 1024 | tf_op jit(solution)/shard_map/while/body/eval_jaxpr/psum | solution.py:121
  175.0 16.9 %psum.24 = f32[128]{0:T(128)S(1)} all-reduce(f32[128]{0:T(128)S(1)} %get-tuple-element.312), channel_id=1, replica_groups=mesh['seq'=64,'head'=8] {'head'}, use_global_device_ids=true, to_apply=%region_5.6 | all-reduce | flops 128 | bytes 1024 | tf_op jit(solution)/shard_map/while/body/eval_jaxpr/psum | solution.py:121
  192.7 1.4 fusion.15
  196.8 503.1 %psum.25 = f32[512]{0:T(512)} all-reduce(f32[512]{0:T(512)S(1)} %bitcast.146), channel_id=1, replica_groups=mesh['seq'=64,'head'=8] {'seq'}, use_global_device_ids=true, to_apply=%region_9.10 | all-reduce | flops 512 | bytes 4096 | tf_op jit(solution)/shard_map/psum | solution.py:203
  700.6 341.5 %while.9 = (s32[]{:T(128)}, f32[4,128,128]{2,1,0:T(8,128)S(1)}, f32[]{:T(128)}, s32[]{:T(128)}, f32[64,4,128,128]{3,2,1,0:T(8,128)}, /*index=5*/f32[64]{0:T(128)...) while((s32[]{:T(128)}, f32[4,128,128]{2,1,0:T(8,128)S(1)}, ...), condition=%wide.region_7.8_spmd, body=%wide.region_6.7_spmd.sunk | while | flops 131088 | bytes 786738 | solution.py:24
  704.4 1.1 bitcast_add_fusion.5
  709.8 1.1 bitcast_add_fusion.5
  715.3 1.1 bitcast_add_fusion.5
  720.7 1.1 bitcast_add_fusion.5
  726.1 1.1 bitcast_add_fusion.5
  731.5 1.1 bitcast_add_fusion.5
  737.0 1.1 bitcast_add_fusion.5
  742.4 1.1 bitcast_add_fusion.5
  747.8 1.1 bitcast_add_fusion.5
  753.2 1.1 bitcast_add_fusion.5
  758.6 1.1 bitcast_add_fusion.5
  764.1 1.1 bitcast_add_fusion.5
  769.5 1.1 bitcast_add_fusion.5
  774.9 1.1 bitcast_add_fusion.5
  780.3 1.1 bitcast_add_fusion.5
  785.7 1.1 bitcast_add_fusion.5
  791.2 1.1 bitcast_add_fusion.5
  796.6 1.1 bitcast_add_fusion.5
  802.0 1.1 bitcast_add_fusion.5
  807.4 1.1 bitcast_add_fusion.5
  812.8 1.1 bitcast_add_fusion.5
  818.3 1.1 bitcast_add_fusion.5
  823.7 1.1 bitcast_add_fusion.5
  829.1 1.1 bitcast_add_fusion.5
  834.5 1.1 bitcast_add_fusion.5
  839.9 1.1 bitcast_add_fusion.5
  845.4 1.1 bitcast_add_fusion.5
  850.8 1.1 bitcast_add_fusion.5
  856.2 1.1 bitcast_add_fusion.5
  861.6 1.1 bitcast_add_fusion.5
  867.0 1.1 bitcast_add_fusion.5
  872.5 1.1 bitcast_add_fusion.5
  877.9 1.1 bitcast_add_fusion.5
  883.3 1.1 bitcast_add_fusion.5
  888.7 1.1 bitcast_add_fusion.5
  894.1 1.1 bitcast_add_fusion.5
  899.6 1.1 bitcast_add_fusion.5
  905.0 1.1 bitcast_add_fusion.5
  915.8 1.1 bitcast_add_fusion.5
  921.2 1.1 bitcast_add_fusion.5
  932.1 1.1 bitcast_add_fusion.5
  937.5 1.1 bitcast_add_fusion.5
  948.4 1.1 bitcast_add_fusion.5
  953.8 1.1 bitcast_add_fusion.5
  964.6 1.1 bitcast_add_fusion.5
  970.0 1.1 bitcast_add_fusion.5
  986.3 1.1 bitcast_add_fusion.5
  991.7 1.1 bitcast_add_fusion.5
  1002.6 1.1 bitcast_add_fusion.5
  1008.0 1.1 bitcast_add_fusion.5
  1018.8 1.1 bitcast_add_fusion.5
  1024.2 1.1 bitcast_add_fusion.5
  1035.1 1.1 bitcast_add_fusion.5
  1040.5 1.1 bitcast_add_fusion.5
  (253 shorter events, 105.7 us)
Async XLA Ops:
  7.2 7.1 copy-start
  7.2 1035.0 %copy-start.3 = (s32[128]{0:T(128)S(1)}, s32[128]{0:T(128)}, u32[]{:S(2)}) copy-start(s32[128]{0:T(128)} %param.14) | copy-start | bytes 1540
  7.2 1036.2 %copy-start.1 = (bf16[128,512]{1,0:T(8,128)(2,1)S(1)}, bf16[128,512]{1,0:T(8,128)(2,1)}, u32[]{:S(2)}) copy-start(bf16[128,512]{1,0:T(8,128)(2,1)} %param.12) | copy-start | bytes 393220
  7.2 1035.0 %copy-start.2 = (f32[4]{0:T(128)S(1)}, f32[4]{0:T(128)}, u32[]{:S(2)}) copy-start(f32[4]{0:T(128)} %param.15) | copy-start | bytes 52
  7.2 145.1 %all-gather.6.cloned.1.call-start = ((), (), s32[]{:S(2)}) async-start(), calls=%async_computation | async-start | bytes 17039360 | tf_op jit(solution)/shard_map/all_gather | solution.py:15
  15.2 685.4 %all-gather.8.cloned.1.call-start = ((), (), s32[]{:S(2)}) async-start(), calls=%async_computation.1 | async-start | bytes 17039360 | tf_op jit(solution)/shard_map/all_gather | solution.py:15
Sparse Core Ops, SparseCore 0:
  15.3 108.7 all-gather.5
  194.2 470.6 all-gather.7
where the time goes:
time: 1060 us; the launch traced here: 1050 us
  blocking collectives  671 us (63%)
  loops' own time  196 us (18%)
  local copies, waits for them, and re-layouts  87 us (8%)
  other arithmetic  75.2 us (7%)
  between operations  14.9 us (1%)
    psum x1, blocking collectives, local(): gain_grad = lax.psum(gain_local, 'seq')  503 us
    another operation x2, loops' own time, prefix_2(): return lax.fori_loop(0, ahead, one, state)  196 us
    unnamed x1, blocking collectives  131 us
    dynamic_slice x126, local copies, waits for them, and re-layouts, one(): lax.dynamic_index_in_dim(a, source, 0, False)  78.2 us
    add x63, other arithmetic, combine_backward(): state_low + factor[:, None, None] * state_high  66.8 us
    psum x2, blocking collectives, forward_step(): square_total, cross_total = lax.psum((square_part, cross_part), 'head')  36.8 us
  transfers between devices with their start and end apart: 2, of which 0 were waited for; matrix products, arithmetic and copies ran while one was open for 1% of the time, Pallas kernels for 0%

commit v1 on v0

--- a/solution.py
+++ b/solution.py
@@ -200,7 +200,7 @@
     _, (key_grad, value_grad) = lax.scan(
         backward_step, (grad_in, next_seg), backward_inputs, reverse=True
     )
-    gain_grad = lax.psum(gain_local, "seq")
+    gain_grad = jnp.sum(lax.all_gather(gain_local, "seq"), axis=0)
     return (
         query_grad,
         key_grad.reshape(tok_rows, heads_here * HEAD_DIM),

time: 1060 us -> 1020 us (0.962)
  blocking collectives: 671 us -> 589 us
  waiting for transfers between devices: 0.07 us -> 45.6 us
    psum x1 -> x0, blocking collectives: 503 us -> none  [local(): gain_grad = lax.psum(gain_local, 'seq')]
    all_gather x0 -> x1, blocking collectives: none -> 421 us  [local(): gain_grad = jnp.sum(lax.all_gather(gain_local, 'seq'), axis=0)]
    all_gather x2, waiting for transfers between devices: 0.04 us -> 45.5 us  [prefix_2(): gathered = jax.tree.map(lambda a: lax.all_gather(a, axis), part)]
  transfers between devices with their start and end apart: 2 -> 2, of which waited for: 0 -> 1; matrix products, arithmetic and copies ran while one was open for 1% -> 1% of each run, Pallas kernels for 0% -> 0%
where the time goes in v1:
time: 1020 us
  blocking collectives  589 us (58%)
  loops' own time  196 us (19%)
  local copies, waits for them, and re-layouts  87.1 us (9%)
  other arithmetic  75.9 us (7%)
  waiting for transfers between devices  45.6 us (4%)
  between operations  14.9 us (1%)
    all_gather x1, blocking collectives, local(): gain_grad = jnp.sum(lax.all_gather(gain_local, 'seq'), axis=0)  421 us
    another operation x2, loops' own time, prefix_2(): return lax.fori_loop(0, ahead, one, state)  196 us
    unnamed x1, blocking collectives  131 us
    dynamic_slice x126, local copies, waits for them, and re-layouts, one(): lax.dynamic_index_in_dim(a, source, 0, False)  78.4 us
    add x63, other arithmetic, combine_backward(): state_low + factor[:, None, None] * state_high  66.8 us
    all_gather x2, waiting for transfers between devices, prefix_2(): gathered = jax.tree.map(lambda a: lax.all_gather(a, axis), part)  45.5 us
    psum x2, blocking collectives, forward_step(): square_total, cross_total = lax.psum((square_part, cross_part), 'head')  36.8 us
  transfers between devices with their start and end apart: 2, of which 1 were waited for; matrix products, arithmetic and copies ran while one was open for 1% of the time, Pallas kernels for 0%

profile of v1, /device:TPU:64, one launch (start us, length us, event | category | flops | bytes accessed | tf_op | source)
XLA Modules:
  0.0 1015.6 jit_solution(15957905365908901342)
XLA Ops:
  9.0 1.3 dynamic-slice.3
  10.3 1.2 fusion.42
  11.5 2.0 broadcast_compare_fusion.1
  18.4 131.0 %all-reduce.3 = (f32[64]{0:T(128)S(1)}, f32[64]{0:T(128)S(1)}, f32[256]{0:T(256)S(1)}) all-reduce(f32[64]{0:T(128)S(1)} %slice_dynamic-update-slice_fusion, f32[64]{0:T(128)S(1)} %get-tuple-element.353, f32[256]{0:T(256)S(1)} %exponential_dynamic-update-slice_fusion), channel_id=1, replica_groups=mesh['seq'=64,'head'=8] {'seq'}, use_global_device_ids=true, to_apply=%add | all-reduce | flops 384 | bytes 3072
  150.7 1.1 convolution_multiply_fusion.1
  154.1 20.0 %psum.16 = f32[128]{0:T(128)S(1)} all-reduce(f32[128]{0:T(128)S(1)} %get-tuple-element.355), channel_id=1, replica_groups=mesh['seq'=64,'head'=8] {'head'}, use_global_device_ids=true, to_apply=%region_3.4 | all-reduce | flops 128 | bytes 1024 | tf_op jit(solution)/shard_map/while/body/eval_jaxpr/psum | solution.py:121
  175.0 16.9 %psum.17 = f32[128]{0:T(128)S(1)} all-reduce(f32[128]{0:T(128)S(1)} %get-tuple-element.312), channel_id=1, replica_groups=mesh['seq'=64,'head'=8] {'head'}, use_global_device_ids=true, to_apply=%region_5.6 | all-reduce | flops 128 | bytes 1024 | tf_op jit(solution)/shard_map/while/body/eval_jaxpr/psum | solution.py:121
  192.7 1.4 fusion.15
  196.8 420.9 %all-gather.3 = f32[64,1,512]{2,1,0:T(1,128)S(1)} all-gather(f32[1,1,512]{2,1,0:T(1,128)S(1)} %bitcast.146), channel_id=1, replica_groups=mesh['seq'=64,'head'=8] {'seq'}, dimensions={0}, use_global_device_ids=true | all-gather | bytes 133120 | tf_op jit(solution)/shard_map/all_gather | solution.py:203
  619.1 45.5 %all-gather.9.cloned.1.call-done = f32[256,128,128]{2,1,0:T(8,128)} async-done(((f32[4,128,128]{2,1,0:T(8,128)}), f32[256,128,128]{2,1,0:T(8,128)}) %all-gather.9.cloned.1.call-update) | async-done | bytes 16777232 | tf_op jit(solution)/shard_map/all_gather | solution.py:15
  664.6 341.6 %while.9 = (s32[]{:T(128)}, f32[4,128,128]{2,1,0:T(8,128)S(1)}, f32[]{:T(128)}, s32[]{:T(128)}, f32[64,4,128,128]{3,2,1,0:T(8,128)}, /*index=5*/f32[64]{0:T(128)...) while((s32[]{:T(128)}, f32[4,128,128]{2,1,0:T(8,128)S(1)}, ...), condition=%wide.region_7.8_spmd, body=%wide.region_6.7_spmd.sunk | while | flops 131088 | bytes 786738 | solution.py:24
  668.4 1.1 bitcast_add_fusion.5
  673.8 1.1 bitcast_add_fusion.5
  679.3 1.1 bitcast_add_fusion.5
  684.7 1.1 bitcast_add_fusion.5
  690.1 1.1 bitcast_add_fusion.5
  695.5 1.1 bitcast_add_fusion.5
  701.0 1.1 bitcast_add_fusion.5
  706.4 1.1 bitcast_add_fusion.5
  711.8 1.1 bitcast_add_fusion.5
  717.2 1.1 bitcast_add_fusion.5
  722.6 1.1 bitcast_add_fusion.5
  728.1 1.1 bitcast_add_fusion.5
  733.5 1.1 bitcast_add_fusion.5
  738.9 1.1 bitcast_add_fusion.5
  744.3 1.1 bitcast_add_fusion.5
  749.8 1.1 bitcast_add_fusion.5
  755.2 1.1 bitcast_add_fusion.5
  760.6 1.1 bitcast_add_fusion.5
  766.0 1.1 bitcast_add_fusion.5
  771.5 1.1 bitcast_add_fusion.5
  776.9 1.1 bitcast_add_fusion.5
  782.3 1.1 bitcast_add_fusion.5
  787.7 1.1 bitcast_add_fusion.5
  793.1 1.1 bitcast_add_fusion.5
  798.6 1.1 bitcast_add_fusion.5
  804.0 1.1 bitcast_add_fusion.5
  809.4 1.1 bitcast_add_fusion.5
  814.8 1.1 bitcast_add_fusion.5
  820.3 1.1 bitcast_add_fusion.5
  825.7 1.1 bitcast_add_fusion.5
  831.1 1.1 bitcast_add_fusion.5
  836.5 1.1 bitcast_add_fusion.5
  841.9 1.1 bitcast_add_fusion.5
  847.4 1.1 bitcast_add_fusion.5
  852.8 1.1 bitcast_add_fusion.5
  858.2 1.1 bitcast_add_fusion.5
  863.6 1.1 bitcast_add_fusion.5
  874.5 1.1 bitcast_add_fusion.5
  885.3 1.1 bitcast_add_fusion.5
  890.8 1.1 bitcast_add_fusion.5
  901.6 1.1 bitcast_add_fusion.5
  912.4 1.1 bitcast_add_fusion.5
  923.3 1.1 bitcast_add_fusion.5
  928.7 1.1 bitcast_add_fusion.5
  939.6 1.1 bitcast_add_fusion.5
  950.4 1.1 bitcast_add_fusion.5
  955.8 1.1 bitcast_add_fusion.5
  961.2 1.1 bitcast_add_fusion.5
  966.7 1.1 bitcast_add_fusion.5
  977.5 1.1 bitcast_add_fusion.5
  988.4 1.1 bitcast_add_fusion.5
  993.8 1.1 bitcast_add_fusion.5
  1004.6 1.1 bitcast_add_fusion.5
  (254 shorter events, 107.6 us)
Async XLA Ops:
  7.2 7.1 copy-start
  7.2 999.1 %copy-start.3 = (s32[128]{0:T(128)S(1)}, s32[128]{0:T(128)}, u32[]{:S(2)}) copy-start(s32[128]{0:T(128)} %param.14) | copy-start | bytes 1540
  7.2 1000.4 %copy-start.1 = (bf16[128,512]{1,0:T(8,128)(2,1)S(1)}, bf16[128,512]{1,0:T(8,128)(2,1)}, u32[]{:S(2)}) copy-start(bf16[128,512]{1,0:T(8,128)(2,1)} %param.12) | copy-start | bytes 393220
  7.2 999.1 %copy-start.2 = (f32[4]{0:T(128)S(1)}, f32[4]{0:T(128)}, u32[]{:S(2)}) copy-start(f32[4]{0:T(128)} %param.15) | copy-start | bytes 52
  7.2 145.1 %all-gather.7.cloned.1.call-start = ((), (), s32[]{:S(2)}) async-start(), calls=%async_computation | async-start | bytes 17039360 | tf_op jit(solution)/shard_map/all_gather | solution.py:15
  15.2 649.4 %all-gather.9.cloned.1.call-start = ((), (), s32[]{:S(2)}) async-start(), calls=%async_computation.1 | async-start | bytes 17039360 | tf_op jit(solution)/shard_map/all_gather | solution.py:15
Sparse Core Ops, SparseCore 0:
  15.3 108.7 all-gather.6
  194.2 470.3 all-gather.8
